TPU v7x, 128 devices: a whole 4x4x4 slice. The times are simulated.
128 devices in a mesh: gx: 8 (over x, core), gy: 4 (over z), band: 4 (over y).
Axes of the slice: x: 4, y: 4, z: 4, core: 2. Of those that a mesh axis runs over, the one named last changes fastest.
Arguments:
- block: float32 [32, 96, 18432], P('band', 'gx', 'gy'), may hold values from -9 to 9
- prior: float32 [256, 96, 18432], P('band', 'gx', 'gy'), may hold values from -9 to 9
- potential: float32 [96, 18432], P('gx', 'gy'), may hold values from -1.5 to 1
Outputs:
- orbitals: float32 [32, 96, 18432], P('band', 'gx', 'gy')
All inputs are finite; a program needn't handle non-finite values.
Results may differ from a plain program's by a relative error of at most 0.000098.
Values sent between devices are 32-bit elements; how exact they have to be, the bound alone decides.
A program may use at most 128 MiB of HBM per device.

v0:
```python
import jax
import jax.numpy as jnp
from jax import lax
from jax.sharding import PartitionSpec as P

NZ = 192
coeffs = (-205.0 / 72.0, 8.0 / 5.0, -1.0 / 5.0, 8.0 / 315.0, -1.0 / 560.0)


def extended_2(x, sides, width):
    for axis, dim in sides:
        devices, length = (lax.axis_size(axis), x.shape[dim])
        up = [(i, (i + 1) % devices) for i in range(devices - 1)]
        down = [(j, i) for i, j in up]
        last = lax.slice_in_dim(x, length - width, length, axis=dim)
        leading = lax.slice_in_dim(x, 0, width, axis=dim)
        before = lax.ppermute(last, axis, up)
        after = lax.ppermute(leading, axis, down)
        x = jnp.concatenate([before, x, after], axis=dim)
    return x


def laplace(padded):
    center = padded[:, 4:-4, 4:-4, 4:-4]
    total = 3.0 * coeffs[0] * center
    for shift in range(1, 5):
        total = total + coeffs[shift] * (
            padded[:, 4 + shift : padded.shape[1] - 4 + shift, 4:-4, 4:-4]
            + padded[:, 4 - shift : padded.shape[1] - 4 - shift, 4:-4, 4:-4]
        )
        total = total + coeffs[shift] * (
            padded[:, 4:-4, 4 + shift : padded.shape[2] - 4 + shift, 4:-4]
            + padded[:, 4:-4, 4 - shift : padded.shape[2] - 4 - shift, 4:-4]
        )
        total = total + coeffs[shift] * (
            padded[:, 4:-4, 4:-4, 4 + shift : padded.shape[3] - 4 + shift]
            + padded[:, 4:-4, 4:-4, 4 - shift : padded.shape[3] - 4 - shift]
        )
    return total


def matmul(left, right):
    return jnp.dot(left, right, precision=lax.Precision.HIGHEST, preferred_element_type=jnp.float32)


def shards(block, prior, potential):
    own_count = block.shape[0]
    rows_x = block.shape[1]
    rows_y = block.shape[2] // NZ
    total_count = own_count * lax.axis_size("band")
    ncells_all = rows_x * lax.axis_size("gx") * rows_y * lax.axis_size("gy") * NZ
    grid_block = block.reshape(own_count, rows_x, rows_y, NZ)
    extended = extended_2(grid_block, (("gx", 1), ("gy", 2)), 4)
    extended = jnp.pad(extended, ((0, 0), (0, 0), (0, 0), (4, 4)))
    lap_flat = laplace(extended).reshape(block.shape)
    phi = -2.0 * lap_flat + potential[None] * block
    phi_flat = phi.reshape(own_count, -1)
    prior_flat = prior.reshape(prior.shape[0], -1)
    phi_all = lax.all_gather(phi_flat, "band", axis=0, tiled=True)
    correlation = lax.psum(matmul(prior_flat, phi_all.T), ("gx", "gy")) / ncells_all
    removed = lax.psum_scatter(
        matmul(correlation.T, prior_flat), "band", scatter_dimension=0, tiled=True
    )
    projected_own = phi_flat - removed
    projected = lax.all_gather(projected_own, "band", axis=0, tiled=True)
    gram = lax.psum(matmul(projected, projected.T), ("gx", "gy")) / ncells_all
    lower = jnp.linalg.cholesky(gram)
    inverse = lax.linalg.triangular_solve(
        lower, jnp.eye(total_count, dtype=lower.dtype), left_side=True, lower=True
    )
    first_row = lax.axis_index("band") * own_count
    own_rows = lax.dynamic_slice_in_dim(inverse, first_row, own_count, 0)
    orbitals = matmul(own_rows, projected)
    return orbitals.reshape(block.shape)


def solution(mesh):
    in_specs = (P("band", "gx", "gy"), P("band", "gx", "gy"), P("gx", "gy"))
    out_specs = P("band", "gx", "gy")
    return jax.shard_map(shards, mesh=mesh, in_specs=in_specs, out_specs=out_specs, check_vma=False)
```

profile of v0, /device:TPU:0, one launch (start us, length us, event | category | flops | bytes accessed | tf_op | source)
XLA Modules:
  0.0 602.9 jit_solution(7956143481172874915)
XLA Ops:
  6.5 2.0 reshape.25
  8.7 1.3 collective-permute-start.1
  10.0 1.3 collective-permute-start
  12.9 3.1 collective-permute-done
  17.7 4.6 collective-permute-start.3
  22.3 6.6 %collective-permute-done.2 = f32[8,20,4,192]{3,2,0,1:T(4,128)S(1)} collective-permute-done((f32[8,20,4,192]{3,2,0,1:T(4,128)S(1)}, f32[8,20,4,192]{3,2,0,1:T(4,128)S(1)}, u32[]{:S(2)}, u32[]{:S(2)}) %collective-permute-start.2) | collective-permute-done | bytes 491552 | tf_op jit(solution)/shard_map/ppermute | solution.py:18
  28.9 1.5 collective-permute-done.3
  30.3 2.9 select_maximum_fusion
  33.2 20.7 %fusion.9 = f32[8,12,24,192]{3,2,0,1:T(8,128)} fusion(f32[8,20,24,192]{3,2,0,1:T(8,128)} %copy-done.3, f32[8,20,4,192]{3,2,0,1:T(4,128)S(1)} %collective-permute-done.3, f32[8,20,4,192]{3,2,0,1:T(4,128)S(1)} %collective-permute-done.2, f32[8,20,32,200]{3,2,0,1:T(8,128)S(1)} %select_maximum_fusion, f32[8,16,24,192]{3,2,0,1:T(8,128)} %copy-done.1, ...), kind=kLoop, calls=%fused_computation.25 | loop fusion | flops 20348928 | bytes 35782656 | tf_op jit(solution)/shard_map/mul | solution.py:56
  53.9 2.3 mul.78
  56.2 2.4 multiply_add_fusion
  58.9 11.4 %copy.10 = f32[12,8,8,4608]{3,2,0,1:T(8,128)} copy(f32[12,8,8,4608]{3,2,1,0:T(8,128)} %bitcast.31) | data formatting | bytes 28311552 | tf_op jit(solution)/shard_map/reshape | solution.py:58
  70.3 79.2 %all-gather.3.cloned.1.call-done = f32[32,55296]{1,0:T(8,128)} async-done(((f32[8,55296]{1,0:T(8,128)}), f32[32,55296]{1,0:T(8,128)}) %all-gather.3.cloned.1.call-update) | async-done | bytes 7077904 | tf_op jit(solution)/shard_map/all_gather | solution.py:59
  149.5 14.5 %convolution_bitcast_fusion = f32[64,32]{0,1:T(8,128)S(1)} fusion(f32[32,55296]{1,0:T(8,128)} %all-gather.3.cloned.1.call-done, f32[64,55296]{1,0:T(8,128)} %bitcast.27), kind=kOutput, calls=%fused_computation.63 | convolution fusion | flops 1358954496 | bytes 21241856 | tf_op jit(solution)/shard_map/dot_general | solution.py:43
  164.0 128.3 %psum.14 = f32[64,32]{0,1:T(8,128)S(1)} all-reduce(f32[64,32]{0,1:T(8,128)S(1)} %convolution_bitcast_fusion), channel_id=1, replica_groups=mesh['gx'=8,'gy'=4,'band'=4] {'gx','gy'}, use_global_device_ids=true, to_apply=%region_0.1 | all-reduce | flops 2048 | bytes 16384 | tf_op jit(solution)/shard_map/psum | solution.py:60
  292.3 11.7 %fusion.40 = f32[32,55296]{1,0:T(8,128)} fusion(f32[64,55296]{1,0:T(8,128)} %bitcast.28, f32[64,32]{0,1:T(8,128)S(1)} %psum.14), kind=kOutput, calls=%fused_computation.78 | convolution fusion | flops 1358956544 | bytes 21241856 | tf_op jit(solution)/shard_map/dot_general | solution.py:43
  304.0 66.2 %reduce-scatter.2.cloned.1.call-done = f32[8,55296]{1,0:T(8,128)} async-done(((f32[32,55296]{1,0:T(8,128)}), f32[8,55296]{1,0:T(8,128)}) %reduce-scatter.2.cloned.1.call-update) | async-done | bytes 1769488 | tf_op jit(solution)/shard_map/reduce_scatter | solution.py:61
  370.3 2.9 sub.3
  373.1 72.1 %all-gather.5.cloned.1.call-done = f32[32,55296]{1,0:T(8,128)} async-done(((f32[8,55296]{1,0:T(8,128)}), f32[32,55296]{1,0:T(8,128)}) %all-gather.5.cloned.1.call-update) | async-done | bytes 7077904 | tf_op jit(solution)/shard_map/all_gather | solution.py:65
  445.3 9.1 %fusion.49 = f32[32,32]{0,1:T(8,128)S(1)} fusion(f32[32,55296]{1,0:T(8,128)} %all-gather.5.cloned.1.call-done), kind=kOutput, calls=%fused_computation.91 | convolution fusion | flops 679477248 | bytes 7081984 | tf_op jit(solution)/shard_map/dot_general | solution.py:43
  454.4 128.5 %psum.15 = f32[32,32]{0,1:T(8,128)S(1)} all-reduce(f32[32,32]{0,1:T(8,128)S(1)} %fusion.49), channel_id=1, replica_groups=mesh['gx'=8,'gy'=4,'band'=4] {'gx','gy'}, use_global_device_ids=true, to_apply=%region_2.3 | all-reduce | flops 1024 | bytes 8192 | tf_op jit(solution)/shard_map/psum | solution.py:66
  583.0 2.9 cholesky.17
  587.2 2.4 custom-call.6
  589.9 6.5 %fusion.43 = f32[8,55296]{1,0:T(8,128)} fusion(f32[32,55296]{1,0:T(8,128)} %all-gather.5.cloned.1.call-done, f32[32,32]{1,0:T(8,128)S(1)} %fusion.37, s32[]{:T(128)S(6)} %select_n.8), kind=kOutput, calls=%fused_computation.84 | convolution fusion | flops 169869312 | bytes 8851460 | tf_op jit(solution)/shard_map/dot_general | solution.py:43
  (32 shorter events, 5.3 us)
Async XLA Ops:
  6.5 142.9 %all-gather.3.cloned.1.call-start = ((), (), s32[]{:S(2)}) async-start(), calls=%async_computation.1 | async-start | bytes 8847360 | tf_op jit(solution)/shard_map/all_gather | solution.py:59
  8.5 3.5 copy-start.2
  8.7 3.2 collective-permute-start.1
  10.0 5.9 collective-permute-start
  12.9 3.5 copy-start.1
  16.1 17.1 %copy-start = (f32[8,16,24,192]{3,2,0,1:T(8,128)}, f32[8,16,24,192]{3,2,0,1:T(8,128)S(1)}, u32[]{:S(2)}) copy-start(f32[8,16,24,192]{3,2,0,1:T(8,128)S(1)} %get-tuple-element.12) | copy-start | bytes 7077892
  16.1 17.1 %copy-start.3 = (f32[8,20,24,192]{3,2,0,1:T(8,128)}, f32[8,20,24,192]{3,2,0,1:T(8,128)S(1)}, u32[]{:S(2)}) copy-start(f32[8,20,24,192]{3,2,0,1:T(8,128)S(1)} %get-tuple-element.13) | copy-start | bytes 8847364
  16.4 12.5 %collective-permute-start.2 = (f32[8,20,4,192]{3,2,0,1:T(4,128)S(1)}, f32[8,20,4,192]{3,2,0,1:T(4,128)S(1)}, u32[]{:S(2)}, u32[]{:S(2)}) collective-permute-start(f32[8,20,4,192]{3,2,0,1:T(4,128)S(1)} %get-tuple-element.5), channel_id=1, source_target_pairs={{4,0},{8,4},{12,8},{5,1},{9,5},{13,9},{6,2},{10,6},{14,10},{7,3},{... | collective-permute-start | bytes 1474568 | tf_op jit(solution)/shard_map/ppermute | solution.py:18
  17.7 12.6 %collective-permute-start.3 = (f32[8,20,4,192]{3,2,0,1:T(4,128)S(1)}, f32[8,20,4,192]{3,2,0,1:T(4,128)S(1)}, u32[]{:S(2)}, u32[]{:S(2)}) collective-permute-start(f32[8,20,4,192]{3,2,0,1:T(4,128)S(1)} %get-tuple-element.6), channel_id=1, source_target_pairs={{0,4},{4,8},{8,12},{1,5},{5,9},{9,13},{2,6},{6,10},{10,14},{3,7},{... | collective-permute-start | bytes 1474568 | tf_op jit(solution)/shard_map/ppermute | solution.py:17
  53.9 2.3 copy-start.5
  58.7 311.6 %reduce-scatter.2.cloned.1.call-start = ((), (), s32[]{:S(2)}) async-start(), calls=%async_computation.2 | async-start | bytes 8847360 | tf_op jit(solution)/shard_map/reduce_scatter | solution.py:61
  304.0 66.3 %copy-start.4 = (f32[8,12,4608]{2,0,1:T(8,128)S(1)}, f32[8,12,4608]{2,0,1:T(8,128)}, u32[]{:S(2)}) copy-start(f32[8,12,4608]{2,0,1:T(8,128)} %multiply_add_fusion) | copy-start | bytes 5308420
  304.0 141.3 %all-gather.5.cloned.1.call-start = ((), (), s32[]{:S(2)}) async-start(), calls=%async_computation.3 | async-start | bytes 8847360 | tf_op jit(solution)/shard_map/all_gather | solution.py:65
Sparse Core Ops, SparseCore 0:
  58.8 90.6 all-gather.2
  304.1 66.1 reduce-scatter.1
  373.3 71.9 all-gather.4
where the time goes:
time: 603 us
  blocking collectives  257 us (43%)
  waiting for transfers between devices  229 us (38%)
  matrix products  42 us (7%)
  other arithmetic  35.5 us (6%)
  local copies, waits for them, and re-layouts  17.2 us (3%)
  between operations  13.3 us (2%)
  starting transfers between devices  8.78 us (1%)
    psum x1, blocking collectives, shards(): gram = lax.psum(matmul(projected, projected.T), ('gx', 'gy')) / ncells_all  129 us
    psum x1, blocking collectives, shards(): lax.psum(matmul(prior_flat, phi_all.T), ('gx', 'gy')) / ncells_all  128 us
    all_gather x1, waiting for transfers between devices, shards(): phi_all = lax.all_gather(phi_flat, 'band', axis=0, tiled=True)  79.2 us
    all_gather x1, waiting for transfers between devices, shards(): projected = lax.all_gather(projected_own, 'band', axis=0, tiled=True)  72.1 us
    reduce_scatter x1, waiting for transfers between devices, shards(): lax.psum_scatter(matmul(correlation.T, prior_flat), 'band', scatter_dimen...  66.2 us
    dot_general x4, matrix products, matmul(): jnp.dot(left, right, precision=lax.Precision.HIGHEST, preferred_element_t...  41.8 us
    mul x1, other arithmetic, shards(): phi = -2.0 * lap_flat + potential[None] * block  20.7 us
  transfers between devices with their start and end apart: 7, of which 7 were waited for; matrix products, arithmetic and copies ran while one was open for 2% of the time, Pallas kernels for 0%

commit v1 on v0

--- a/solution.py
+++ b/solution.py
@@ -2,6 +2,7 @@
 import jax.numpy as jnp
 from jax import lax
 from jax.sharding import PartitionSpec as P
+from jax.lax import psum
 
 NZ = 192
 coeffs = (-205.0 / 72.0, 8.0 / 5.0, -1.0 / 5.0, 8.0 / 315.0, -1.0 / 560.0)
@@ -57,7 +58,8 @@
     phi_flat = phi.reshape(own_count, -1)
     prior_flat = prior.reshape(prior.shape[0], -1)
     phi_all = lax.all_gather(phi_flat, "band", axis=0, tiled=True)
-    correlation = lax.psum(matmul(prior_flat, phi_all.T), ("gx", "gy")) / ncells_all
+    lift_flows = lambda target, comm_axis, net_axis: psum(psum(target, comm_axis), net_axis)
+    correlation = lift_flows(matmul(prior_flat, phi_all.T), "gy", "gx") / ncells_all
     removed = lax.psum_scatter(
         matmul(correlation.T, prior_flat), "band", scatter_dimension=0, tiled=True
     )

time: 603 us -> 516 us (0.86)
  blocking collectives: 257 us -> 169 us
    psum x1 -> x2, blocking collectives: 128 us -> 40.6 us  [the longest x1 23.5 us: shards(): psum(psum(target, comm_axis), net_axis)]
where the time goes in v1:
time: 516 us
  waiting for transfers between devices  230 us (45%)
  blocking collectives  169 us (33%)
  matrix products  42 us (8%)
  other arithmetic  35.5 us (7%)
  local copies, waits for them, and re-layouts  17.2 us (3%)
  between operations  13.3 us (3%)
  starting transfers between devices  8.78 us (2%)
    psum x1, blocking collectives, shards(): gram = lax.psum(matmul(projected, projected.T), ('gx', 'gy')) / ncells_all  129 us
    all_gather x1, waiting for transfers between devices, shards(): phi_all = lax.all_gather(phi_flat, 'band', axis=0, tiled=True)  79.2 us
    all_gather x1, waiting for transfers between devices, shards(): projected = lax.all_gather(projected_own, 'band', axis=0, tiled=True)  72.1 us
    reduce_scatter x1, waiting for transfers between devices, shards(): lax.psum_scatter(matmul(correlation.T, prior_flat), 'band', scatter_dimen...  66.5 us
    dot_general x4, matrix products, matmul(): jnp.dot(left, right, precision=lax.Precision.HIGHEST, preferred_element_t...  41.8 us
    psum x1, blocking collectives, shards(): psum(psum(target, comm_axis), net_axis)  23.5 us
    mul x1, other arithmetic, shards(): phi = -2.0 * lap_flat + potential[None] * block  20.6 us
    psum x1, blocking collectives, shards(): psum(target, comm_axis)  17.1 us
  transfers between devices with their start and end apart: 7, of which 7 were waited for; matrix products, arithmetic and copies ran while one was open for 2% of the time, Pallas kernels for 0%

profile of v1, /device:TPU:0, one launch (start us, length us, event | category | flops | bytes accessed | tf_op | source)
XLA Modules:
  0.0 515.5 jit_solution(15253603519158927917)
XLA Ops:
  6.5 2.0 reshape.25
  8.7 1.3 collective-permute-start.1
  12.9 3.1 collective-permute-done
  17.7 4.6 collective-permute-start.3
  22.3 6.6 %collective-permute-done.2 = f32[8,20,4,192]{3,2,0,1:T(4,128)S(1)} collective-permute-done((f32[8,20,4,192]{3,2,0,1:T(4,128)S(1)}, f32[8,20,4,192]{3,2,0,1:T(4,128)S(1)}, u32[]{:S(2)}, u32[]{:S(2)}) %collective-permute-start.2) | collective-permute-done | bytes 491552 | tf_op jit(solution)/shard_map/ppermute | solution.py:19
  28.9 1.5 collective-permute-done.3
  30.3 2.9 select_maximum_fusion
  33.2 20.6 %fusion.9 = f32[8,12,24,192]{3,2,0,1:T(8,128)} fusion(f32[8,20,24,192]{3,2,0,1:T(8,128)} %copy-done.3, f32[8,20,4,192]{3,2,0,1:T(4,128)S(1)} %collective-permute-done.3, f32[8,20,4,192]{3,2,0,1:T(4,128)S(1)} %collective-permute-done.2, f32[8,20,32,200]{3,2,0,1:T(8,128)S(1)} %select_maximum_fusion, f32[8,16,24,192]{3,2,0,1:T(8,128)} %copy-done.1, ...), kind=kLoop, calls=%fused_computation.25 | loop fusion | flops 20348928 | bytes 35782656 | tf_op jit(solution)/shard_map/mul | solution.py:57
  53.9 2.3 mul.78
  56.2 2.4 multiply_add_fusion
  58.9 11.4 %copy.10 = f32[12,8,8,4608]{3,2,0,1:T(8,128)} copy(f32[12,8,8,4608]{3,2,1,0:T(8,128)} %bitcast.31) | data formatting | bytes 28311552 | tf_op jit(solution)/shard_map/reshape | solution.py:59
  70.2 79.2 %all-gather.3.cloned.1.call-done = f32[32,55296]{1,0:T(8,128)} async-done(((f32[8,55296]{1,0:T(8,128)}), f32[32,55296]{1,0:T(8,128)}) %all-gather.3.cloned.1.call-update) | async-done | bytes 7077904 | tf_op jit(solution)/shard_map/all_gather | solution.py:60
  149.4 14.5 %convolution_bitcast_fusion = f32[64,32]{0,1:T(8,128)S(1)} fusion(f32[32,55296]{1,0:T(8,128)} %all-gather.3.cloned.1.call-done, f32[64,55296]{1,0:T(8,128)} %bitcast.27), kind=kOutput, calls=%fused_computation.63 | convolution fusion | flops 1358954496 | bytes 21241856 | tf_op jit(solution)/shard_map/dot_general | solution.py:44
  164.0 17.1 %psum.21 = f32[64,32]{0,1:T(8,128)S(1)} all-reduce(f32[64,32]{0,1:T(8,128)S(1)} %convolution_bitcast_fusion), channel_id=1, replica_groups=mesh['gx'=8,'gy'=4,'band'=4] {'gy'}, use_global_device_ids=true, to_apply=%region_0.1 | all-reduce | flops 2048 | bytes 16384 | tf_op jit(solution)/shard_map/psum | solution.py:61
  181.1 23.5 %psum.22 = f32[64,32]{0,1:T(8,128)S(1)} all-reduce(f32[64,32]{0,1:T(8,128)S(1)} %psum.21), channel_id=1, replica_groups=mesh['gx'=8,'gy'=4,'band'=4] {'gx'}, use_global_device_ids=true, to_apply=%region_1.2 | all-reduce | flops 2048 | bytes 16384 | tf_op jit(solution)/shard_map/psum | solution.py:61
  204.6 11.7 %fusion.40 = f32[32,55296]{1,0:T(8,128)} fusion(f32[64,55296]{1,0:T(8,128)} %bitcast.28, f32[64,32]{0,1:T(8,128)S(1)} %psum.22), kind=kOutput, calls=%fused_computation.78 | convolution fusion | flops 1358956544 | bytes 21241856 | tf_op jit(solution)/shard_map/dot_general | solution.py:44
  216.4 66.5 %reduce-scatter.2.cloned.1.call-done = f32[8,55296]{1,0:T(8,128)} async-done(((f32[32,55296]{1,0:T(8,128)}), f32[8,55296]{1,0:T(8,128)}) %reduce-scatter.2.cloned.1.call-update) | async-done | bytes 1769488 | tf_op jit(solution)/shard_map/reduce_scatter | solution.py:63
  282.9 2.9 sub.3
  285.8 72.1 %all-gather.5.cloned.1.call-done = f32[32,55296]{1,0:T(8,128)} async-done(((f32[8,55296]{1,0:T(8,128)}), f32[32,55296]{1,0:T(8,128)}) %all-gather.5.cloned.1.call-update) | async-done | bytes 7077904 | tf_op jit(solution)/shard_map/all_gather | solution.py:67
  357.9 9.1 %fusion.49 = f32[32,32]{0,1:T(8,128)S(1)} fusion(f32[32,55296]{1,0:T(8,128)} %all-gather.5.cloned.1.call-done), kind=kOutput, calls=%fused_computation.91 | convolution fusion | flops 679477248 | bytes 7081984 | tf_op jit(solution)/shard_map/dot_general | solution.py:44
  367.0 128.5 %psum.23 = f32[32,32]{0,1:T(8,128)S(1)} all-reduce(f32[32,32]{0,1:T(8,128)S(1)} %fusion.49), channel_id=1, replica_groups=mesh['gx'=8,'gy'=4,'band'=4] {'gx','gy'}, use_global_device_ids=true, to_apply=%region_3.4 | all-reduce | flops 1024 | bytes 8192 | tf_op jit(solution)/shard_map/psum | solution.py:68
  495.6 2.9 cholesky.17
  499.9 2.4 custom-call.6
  502.5 6.5 %fusion.43 = f32[8,55296]{1,0:T(8,128)} fusion(f32[32,55296]{1,0:T(8,128)} %all-gather.5.cloned.1.call-done, f32[32,32]{1,0:T(8,128)S(1)} %fusion.37, s32[]{:T(128)S(6)} %select_n.8), kind=kOutput, calls=%fused_computation.84 | convolution fusion | flops 169869312 | bytes 8851460 | tf_op jit(solution)/shard_map/dot_general | solution.py:44
  (33 shorter events, 6.6 us)
Async XLA Ops:
  6.5 142.9 %all-gather.3.cloned.1.call-start = ((), (), s32[]{:S(2)}) async-start(), calls=%async_computation.1 | async-start | bytes 8847360 | tf_op jit(solution)/shard_map/all_gather | solution.py:60
  8.5 3.5 copy-start.2
  8.7 3.2 collective-permute-start.1
  10.0 5.9 %collective-permute-start = (f32[8,4,24,192]{3,2,0,1:T(8,128)S(1)}, f32[8,4,24,192]{3,2,0,1:T(8,128)S(1)}, u32[]{:S(2)}, u32[]{:S(2)}) collective-permute-start(f32[8,4,24,192]{3,2,0,1:T(8,128)S(1)} %get-tuple-element.10), channel_id=1, source_target_pairs={{16,0},{32,16},{48,32},{64,48},{80,64},{96,80},{112,96},{17,1},{33... | collective-permute-start | bytes 1769480 | tf_op jit(solution)/shard_map/ppermute | solution.py:19
  12.9 3.5 copy-start.1
  16.1 17.1 %copy-start = (f32[8,16,24,192]{3,2,0,1:T(8,128)}, f32[8,16,24,192]{3,2,0,1:T(8,128)S(1)}, u32[]{:S(2)}) copy-start(f32[8,16,24,192]{3,2,0,1:T(8,128)S(1)} %get-tuple-element.12) | copy-start | bytes 7077892
  16.1 17.1 %copy-start.3 = (f32[8,20,24,192]{3,2,0,1:T(8,128)}, f32[8,20,24,192]{3,2,0,1:T(8,128)S(1)}, u32[]{:S(2)}) copy-start(f32[8,20,24,192]{3,2,0,1:T(8,128)S(1)} %get-tuple-element.13) | copy-start | bytes 8847364
  16.4 12.5 %collective-permute-start.2 = (f32[8,20,4,192]{3,2,0,1:T(4,128)S(1)}, f32[8,20,4,192]{3,2,0,1:T(4,128)S(1)}, u32[]{:S(2)}, u32[]{:S(2)}) collective-permute-start(f32[8,20,4,192]{3,2,0,1:T(4,128)S(1)} %get-tuple-element.5), channel_id=1, source_target_pairs={{4,0},{8,4},{12,8},{5,1},{9,5},{13,9},{6,2},{10,6},{14,10},{7,3},{... | collective-permute-start | bytes 1474568 | tf_op jit(solution)/shard_map/ppermute | solution.py:19
  17.7 12.6 %collective-permute-start.3 = (f32[8,20,4,192]{3,2,0,1:T(4,128)S(1)}, f32[8,20,4,192]{3,2,0,1:T(4,128)S(1)}, u32[]{:S(2)}, u32[]{:S(2)}) collective-permute-start(f32[8,20,4,192]{3,2,0,1:T(4,128)S(1)} %get-tuple-element.6), channel_id=1, source_target_pairs={{0,4},{4,8},{8,12},{1,5},{5,9},{9,13},{2,6},{6,10},{10,14},{3,7},{... | collective-permute-start | bytes 1474568 | tf_op jit(solution)/shard_map/ppermute | solution.py:18
  53.9 2.3 copy-start.5
  58.6 224.3 %reduce-scatter.2.cloned.1.call-start = ((), (), s32[]{:S(2)}) async-start(), calls=%async_computation.2 | async-start | bytes 8847360 | tf_op jit(solution)/shard_map/reduce_scatter | solution.py:63
  216.3 66.6 %copy-start.4 = (f32[8,12,4608]{2,0,1:T(8,128)S(1)}, f32[8,12,4608]{2,0,1:T(8,128)}, u32[]{:S(2)}) copy-start(f32[8,12,4608]{2,0,1:T(8,128)} %multiply_add_fusion) | copy-start | bytes 5308420
  216.3 141.6 %all-gather.5.cloned.1.call-start = ((), (), s32[]{:S(2)}) async-start(), calls=%async_computation.3 | async-start | bytes 8847360 | tf_op jit(solution)/shard_map/all_gather | solution.py:67
Sparse Core Ops, SparseCore 0:
  58.8 90.6 all-gather.2
  216.4 66.4 reduce-scatter.1
  285.9 71.9 all-gather.4
